TPU v7x, 256 devices: a whole 4x4x8 slice. The times are simulated.
256 devices in a mesh: row: 32 (over y, x, z_hi), col: 8 (over z_lo, core).
Axes of the slice: x: 4, y: 4, z: 8 (z_hi: 2, z_lo: 4; z = z_hi * 4 + z_lo), core: 2. Of those that a mesh axis runs over, the one named last changes fastest.
Arguments:
- alignment: bfloat16 [64, 1536, 256], P('row', 'col'), may hold values from -6 to 6
- pair_act: bfloat16 [1536, 1536, 128], P('row', 'col'), may hold values from -600 to 600
- targets: int32 [1536, 1536], P('row', 'col'), may hold values from 0 to 63, as said below
- crop_mask: int32 [1536], replicated, may hold values 0 or 1
- projection_weight: bfloat16 [256, 64], replicated, may hold values from -0.375 to 0.375
- w_outer: bfloat16 [1024, 128], replicated, may hold values from -1.5 to 1.5
- w_expand: bfloat16 [128, 512], replicated, may hold values from -0.5 to 0.5
- w_shrink: bfloat16 [512, 128], replicated, may hold values from -0.25 to 0.25
- w_bins: bfloat16 [128, 64], replicated, may hold values from -1.8 to 1.8
Outputs:
- pair_grad: bfloat16 [1536, 1536, 128], P('row', 'col')
Inputs may be any that keep to these rules, and one draw needn't show every extreme that they name: targets[i, j] equals targets[j, i].
All inputs are finite; a program needn't handle non-finite values.
Results may differ from a plain program's by a relative error of at most 0.02.
The roundings to bfloat16 on the way count: a program that leaves them out, or rounds other values in their place, can miss the bound.
Values may be sent and summed in bfloat16 or wider, within the bound.
A program may use at most 128 MiB of HBM per device.

v0:
```python
import jax
import jax.numpy as jnp
from jax import lax
from jax.sharding import PartitionSpec as P

FACTOR_CHANNELS = 32
BINS = 64
SEQUENCE_COUNT = 64
epsilon = 1e-05


def from_root(shard, axis, root):
    mine = lax.axis_index(axis) == root
    return lax.psum(jnp.where(mine, shard, jnp.zeros_like(shard)), axis)


def layer_normalize(values):
    average = jnp.mean(values, axis=-1, keepdims=True)
    centred = values - average
    inverse_deviation = lax.rsqrt(jnp.mean(centred * centred, axis=-1, keepdims=True) + epsilon)
    return (centred * inverse_deviation, inverse_deviation)


def norm_project(shard_rows, projection_weight):
    normed = layer_normalize(shard_rows.astype(jnp.float32))[0].astype(jnp.bfloat16)
    factor = jnp.dot(normed, projection_weight, preferred_element_type=jnp.float32).astype(
        jnp.bfloat16
    )
    return factor.reshape(shard_rows.shape[0], -1)


def mirrored(tile_rows, rows_dev, n_row, n_col):
    ratio = n_row // n_col
    group_rows = tile_rows.shape[0] // n_col
    sectioned = tile_rows.reshape(n_col, group_rows, ratio, rows_dev * BINS).transpose(0, 2, 1, 3)
    first_hop = lax.all_to_all(sectioned, "col", split_axis=0, concat_axis=0, tiled=True)
    regrouped = first_hop.reshape(n_row, 1, group_rows, rows_dev * BINS)
    arrived = lax.all_to_all(
        lax.all_to_all(regrouped, "row", split_axis=0, concat_axis=1, tiled=True),
        "col",
        split_axis=1,
        concat_axis=0,
        tiled=True,
    )
    return arrived.reshape(n_col, ratio, group_rows, rows_dev, BINS).transpose(3, 1, 0, 2, 4)


def per_device(
    alignment, pair_act, targets, crop_mask, projection_weight, w_outer, w_expand, w_shrink, w_bins
):
    rows_dev, cols_dev, channels = pair_act.shape
    n_row = lax.axis_size("row")
    n_col = lax.axis_size("col")
    ratio = n_row // n_col
    row_index = lax.axis_index("row")
    col_index = lax.axis_index("col")
    factors = norm_project(lax.all_gather(alignment, "row", axis=0, tiled=True), projection_weight)
    factors = factors.reshape(SEQUENCE_COUNT, cols_dev, 2 * FACTOR_CHANNELS)
    right_side = factors[:, :, FACTOR_CHANNELS:]
    own_left = lax.dynamic_slice_in_dim(
        factors[:, :, :FACTOR_CHANNELS], row_index % ratio * rows_dev, rows_dev, 1
    )
    left_side = from_root(
        own_left.reshape(SEQUENCE_COUNT, rows_dev * FACTOR_CHANNELS), "col", row_index // ratio
    )
    left_side = left_side.reshape(SEQUENCE_COUNT, rows_dev, FACTOR_CHANNELS)
    block_rows = 8
    blocks = rows_dev // block_rows
    pair_blocks = pair_act.reshape(blocks, block_rows, cols_dev, channels)
    left_blocks = left_side.reshape(SEQUENCE_COUNT, blocks, block_rows, FACTOR_CHANNELS).transpose(
        1, 0, 2, 3
    )

    def forward_block(inputs):
        pair_rows, left_rows = inputs
        outer = (
            jnp.einsum("sic,sje->ijce", left_rows, right_side, preferred_element_type=jnp.float32)
            / SEQUENCE_COUNT
        )
        outer = outer.reshape(block_rows * cols_dev, FACTOR_CHANNELS * FACTOR_CHANNELS).astype(
            jnp.bfloat16
        )
        update = jnp.dot(outer, w_outer, preferred_element_type=jnp.float32)
        middle_state = (
            pair_rows.reshape(block_rows * cols_dev, channels).astype(jnp.float32) + update
        ).astype(jnp.bfloat16)
        xnorm = layer_normalize(middle_state.astype(jnp.float32))[0].astype(jnp.bfloat16)
        before = lax.optimization_barrier(
            jnp.dot(xnorm, w_expand, preferred_element_type=jnp.float32).astype(jnp.bfloat16)
        )
        hidden = jax.nn.silu(before.astype(jnp.float32)).astype(jnp.bfloat16)
        final = (
            middle_state.astype(jnp.float32)
            + jnp.dot(hidden, w_shrink, preferred_element_type=jnp.float32)
        ).astype(jnp.bfloat16)
        logits = jnp.dot(final, w_bins, preferred_element_type=jnp.float32).astype(jnp.bfloat16)
        return (middle_state, before, logits.reshape(block_rows, cols_dev * BINS))

    middle_state, before, logits = lax.map(forward_block, (pair_blocks, left_blocks))
    across = mirrored(logits.reshape(rows_dev, cols_dev * BINS), rows_dev, n_row, n_col).reshape(
        rows_dev, cols_dev, BINS
    )
    own = logits.reshape(rows_dev, cols_dev, BINS)
    scores = own.astype(jnp.float32) + across.astype(jnp.float32)
    scores = scores - jnp.max(scores, axis=-1, keepdims=True)
    expo = jnp.exp(scores)
    prob = expo / jnp.sum(expo, axis=-1, keepdims=True)
    onehot = (targets[:, :, None] == jnp.arange(BINS, dtype=jnp.int32)).astype(jnp.float32)
    row_mask = lax.dynamic_slice_in_dim(crop_mask, row_index * rows_dev, rows_dev).astype(
        jnp.float32
    )
    col_mask = lax.dynamic_slice_in_dim(crop_mask, col_index * cols_dev, cols_dev).astype(
        jnp.float32
    )
    weight = row_mask[:, None] * col_mask[None, :]
    dlogits = (2.0 * (prob - onehot) * weight[:, :, None]).astype(jnp.bfloat16)
    dlog_blocks = dlogits.reshape(blocks, block_rows * cols_dev, BINS)

    def backward_block(inputs):
        middle_row_block, before_rows, dlog_rows = inputs
        final_gradient = jnp.dot(dlog_rows, w_bins.T, preferred_element_type=jnp.float32)
        before_f = before_rows.astype(jnp.float32)
        sigma = jax.nn.sigmoid(before_f)
        slope = sigma * (1.0 + before_f * (1.0 - sigma))
        dhidden = (
            jnp.dot(
                final_gradient.astype(jnp.bfloat16), w_shrink.T, preferred_element_type=jnp.float32
            )
            * slope
        ).astype(jnp.bfloat16)
        normed_input_gradient = jnp.dot(dhidden, w_expand.T, preferred_element_type=jnp.float32)
        standardized_input, inverse_deviation = layer_normalize(
            middle_row_block.astype(jnp.float32)
        )
        middle_gradient = final_gradient + inverse_deviation * (
            normed_input_gradient
            - jnp.mean(normed_input_gradient, axis=-1, keepdims=True)
            - standardized_input
            * jnp.mean(normed_input_gradient * standardized_input, axis=-1, keepdims=True)
        )
        return middle_gradient.astype(jnp.bfloat16)

    grads = lax.map(backward_block, (middle_state, before, dlog_blocks))
    return grads.reshape(rows_dev, cols_dev, channels)


def solution(mesh):
    in_specs = (
        P("row", "col", None),
        P("row", "col", None),
        P("row", "col"),
        P(),
        P(),
        P(),
        P(),
        P(),
        P(),
    )
    out_specs = P("row", "col", None)
    return jax.shard_map(
        per_device, mesh=mesh, in_specs=in_specs, out_specs=out_specs, check_vma=False
    )
```

profile of v0, /device:TPU:1, one launch (start us, length us, event | category | flops | bytes accessed | tf_op | source)
XLA Modules:
  0.0 618.3 jit_solution(1737578397463702173)
XLA Ops:
  7.3 138.0 %all-gather.2.cloned.1.call-done = bf16[64,192,256]{2,1,0:T(8,128)(2,1)} async-done(((bf16[2,192,256]{2,1,0:T(8,128)(2,1)}), bf16[64,192,256]{2,1,0:T(8,128)(2,1)}) %all-gather.2.cloned.1.call-update) | async-done | bytes 6291472 | tf_op jit(solution)/shard_map/all_gather | solution.py:57
  145.3 5.2 convert_reduce_fusion.2
  150.5 4.4 fusion.54
  155.0 5.2 fusion.60
  164.0 62.7 %all-reduce.2.cloned.1.call-done = bf16[6,64,8,32]{1,3,2,0:T(8,128)(2,1)} async-done(((bf16[6,64,8,32]{1,3,2,0:T(8,128)(2,1)}), bf16[6,64,8,32]{1,3,2,0:T(8,128)(2,1)}) %all-reduce.2.cloned.1.call-update) | async-done | bytes 196624 | tf_op jit(solution)/shard_map/psum | solution.py:14
  226.7 158.3 %while.24 = (s32[]{:T(128)}, bf16[6,1536,128]{1,2,0:T(8,128)(2,1)}, bf16[6,1536,512]{2,1,0:T(8,128)(2,1)}, bf16[6,8,12288]{2,1,0:T(8,128)(2,1)}, bf16[6,8,192,12...) while((s32[]{:T(128)}, bf16[6,1536,128]{1,2,0:T(8,128)(2,1)}, ...), condition=%wide.region_6.7_spmd, body=%wide.region_3.6_spmd.sunk | while | flops 1043695104 | bytes 37036208 | solution.py:99
  226.7 2.5 fusion.107
  229.2 4.5 copy.80
  233.7 6.3 %convert_element_type.284 = bf16[1536,1024]{0,1:T(8,128)(2,1)S(1)} reshape(bf16[8,192,32,32]{1,0,3,2:T(8,128)(2,1)} %copy.80) | data formatting | bytes 6291456 | tf_op jit(solution)/shard_map/while/body/eval_jaxpr/convert_element_type | solution.py:80
  242.0 2.3 copy.79
  244.3 2.6 bitcast_dynamic-update-slice_fusion.4
  248.3 2.3 convolution_convert_fusion.5
  253.1 2.5 fusion.107
  255.6 4.5 copy.80
  260.1 6.3 %convert_element_type.284 = bf16[1536,1024]{0,1:T(8,128)(2,1)S(1)} reshape(bf16[8,192,32,32]{1,0,3,2:T(8,128)(2,1)} %copy.80) | data formatting | bytes 6291456 | tf_op jit(solution)/shard_map/while/body/eval_jaxpr/convert_element_type | solution.py:80
  268.4 2.3 copy.79
  270.7 2.6 bitcast_dynamic-update-slice_fusion.4
  274.6 2.3 convolution_convert_fusion.5
  279.5 2.5 fusion.107
  282.0 4.5 copy.80
  286.5 6.3 %convert_element_type.284 = bf16[1536,1024]{0,1:T(8,128)(2,1)S(1)} reshape(bf16[8,192,32,32]{1,0,3,2:T(8,128)(2,1)} %copy.80) | data formatting | bytes 6291456 | tf_op jit(solution)/shard_map/while/body/eval_jaxpr/convert_element_type | solution.py:80
  294.8 2.3 copy.79
  297.1 2.6 bitcast_dynamic-update-slice_fusion.4
  301.0 2.3 convolution_convert_fusion.5
  305.9 2.5 fusion.107
  308.3 4.5 copy.80
  312.8 6.3 %convert_element_type.284 = bf16[1536,1024]{0,1:T(8,128)(2,1)S(1)} reshape(bf16[8,192,32,32]{1,0,3,2:T(8,128)(2,1)} %copy.80) | data formatting | bytes 6291456 | tf_op jit(solution)/shard_map/while/body/eval_jaxpr/convert_element_type | solution.py:80
  321.1 2.3 copy.79
  323.4 2.6 bitcast_dynamic-update-slice_fusion.4
  327.3 2.3 convolution_convert_fusion.5
  332.2 2.5 fusion.107
  334.7 4.5 copy.80
  339.2 6.3 %convert_element_type.284 = bf16[1536,1024]{0,1:T(8,128)(2,1)S(1)} reshape(bf16[8,192,32,32]{1,0,3,2:T(8,128)(2,1)} %copy.80) | data formatting | bytes 6291456 | tf_op jit(solution)/shard_map/while/body/eval_jaxpr/convert_element_type | solution.py:80
  347.5 2.3 copy.79
  349.8 2.5 bitcast_dynamic-update-slice_fusion.4
  353.7 2.3 convolution_convert_fusion.5
  358.6 2.5 fusion.107
  361.1 4.5 copy.80
  365.6 6.3 %convert_element_type.284 = bf16[1536,1024]{0,1:T(8,128)(2,1)S(1)} reshape(bf16[8,192,32,32]{1,0,3,2:T(8,128)(2,1)} %copy.80) | data formatting | bytes 6291456 | tf_op jit(solution)/shard_map/while/body/eval_jaxpr/convert_element_type | solution.py:80
  373.9 2.3 copy.79
  376.1 2.6 bitcast_dynamic-update-slice_fusion.4
  380.1 2.3 convolution_convert_fusion.5
  385.0 2.0 reshape_reshape.7
  387.0 34.3 %all_to_all.26 = bf16[8,4,6,3072]{3,1,2,0:T(4,128)(2,1)S(1)} all-to-all(bf16[8,4,6,3072]{3,1,2,0:T(4,128)(2,1)S(1)} %bitcast.140), channel_id=1, replica_groups=mesh['row'=32,'col'=8] {'col'}, dimensions={0} | all-to-all | bytes 2359296 | tf_op jit(solution)/shard_map/all_to_all | solution.py:36
  421.7 50.7 %all_to_all.27 = bf16[32,1,6,3072]{3,2,1,0:T(8,128)(2,1)} all-to-all(bf16[32,1,6,3072]{3,2,1,0:T(8,128)(2,1)S(1)} %bitcast.139), channel_id=1, replica_groups=mesh['row'=32,'col'=8] {'row'}, dimensions={0} | all-to-all | bytes 2359296 | tf_op jit(solution)/shard_map/all_to_all | solution.py:39
  472.4 7.7 %all-to-all-start.2 = ((bf16[1,32,6,3072]{3,2,0,1:T(8,128)(2,1)}), bf16[1,32,6,3072]{3,2,0,1:T(8,128)(2,1)}, u32[]{:S(2)}, u32[]{:S(2)}) async-start(bf16[1,32,6,3072]{3,2,0,1:T(8,128)(2,1)} %bitcast.20), calls=%async_computation.2 | async-start | bytes 3145728 | tf_op jit(solution)/shard_map/all_to_all | solution.py:38
  482.1 3.6 reshape.139
  485.8 3.5 reshape.137
  489.3 27.8 %all-to-all-done.2 = bf16[1,32,6,3072]{3,2,0,1:T(8,128)(2,1)} async-done(((bf16[1,32,6,3072]{3,2,0,1:T(8,128)(2,1)}), bf16[1,32,6,3072]{3,2,0,1:T(8,128)(2,1)}, u32[]{:S(2)}, u32[]{:S(2)}) %all-to-all-start.2) | async-done | bytes 1179680 | tf_op jit(solution)/shard_map/all_to_all | solution.py:38
  517.1 2.1 copy_convert_fusion
  519.2 3.2 reshape.141
  522.4 3.0 copy.60
  526.1 2.4 fusion.63
  528.6 4.7 exponential_reduce_fusion
  533.3 7.9 %copy.59 = f32[48,4,8,6,64]{4,3,2,1,0:T(8,128)} copy(f32[48,4,8,6,64]{4,0,1,2,3:T(8,128)} %bitcast.138) | data formatting | bytes 4718592 | tf_op jit(solution)/shard_map/convert_element_type | solution.py:104
  541.3 6.6 %reshape.138 = f32[6,1536,64]{2,1,0:T(8,128)} reshape(f32[48,4,8,6,64]{4,3,2,1,0:T(8,128)} %copy.59) | data formatting | bytes 4718592 | tf_op jit(solution)/shard_map/convert_element_type | solution.py:104
  547.9 8.4 %multiply_convert_fusion.1 = bf16[6,1536,64]{2,1,0:T(8,128)(2,1)} fusion(f32[6,1536,64]{2,1,0:T(8,128)} %reshape.137, f32[6,1536,64]{2,1,0:T(8,128)} %reshape.138, f32[6,1536]{1,0:T(8,128)S(1)} %multiply_multiply_fusion, s32[6,1536]{1,0:T(8,128)S(1)} %eq.22, f32[6,1536]{1,0:T(8,128)S(1)} %div.58, f32[6,1536]{1,0:T(8,128)S(1)} %sub.64), kind=kLoop, calls=%fused_computation.82 | loop fusion | flops 4718592 | bytes 6045696 | tf_op jit(solution)/shard_map/convert_element_type | solution.py:116
  556.3 54.4 %while.25 = (s32[]{:T(128)}, bf16[6,1536,128]{2,1,0:T(8,128)(2,1)}, bf16[6,1536,64]{2,1,0:T(8,128)(2,1)}, bf16[128,64]{0,1:T(8,128)(2,1)S(1)}, bf16[6,1536,128]{...) while((s32[]{:T(128)}, bf16[6,1536,128]{2,1,0:T(8,128)(2,1)}, ...), condition=%wide.region_14.15_spmd, body=%wide.region_9.14_spmd.sunk | while | flops 440010240 | bytes 12193377 | solution.py:143
  559.8 2.9 fusion.115
  568.8 3.0 fusion.115
  577.8 2.9 fusion.115
  586.8 3.0 fusion.115
  595.8 2.9 fusion.115
  604.8 3.0 fusion.115
  (205 shorter events, 79.7 us)
Async XLA Ops:
  6.5 148.5 %copy-start = (bf16[256,64]{0,1:T(8,128)(2,1)S(1)}, bf16[256,64]{0,1:T(8,128)(2,1)}, u32[]{:S(2)}) copy-start(bf16[256,64]{0,1:T(8,128)(2,1)} %param.17) | copy-start | bytes 98308
  6.5 138.8 %all-gather.2.cloned.1.call-start = ((), (), s32[]{:S(2)}) async-start(), calls=%async_computation.3 | async-start | bytes 6488064 | tf_op jit(solution)/shard_map/all_gather | solution.py:57
  7.3 219.5 %all-reduce.2.cloned.1.call-start = ((), (), s32[]{:S(2)}) async-start(), calls=%async_computation.4 | async-start | bytes 786432 | tf_op jit(solution)/shard_map/psum | solution.py:14
  145.3 5.2 copy-start.3
  160.4 66.3 %copy-start.5 = (bf16[1024,128]{1,0:T(8,128)(2,1)S(1)}, bf16[1024,128]{1,0:T(8,128)(2,1)}, u32[]{:S(2)}) copy-start(bf16[1024,128]{1,0:T(8,128)(2,1)} %param.18) | copy-start | bytes 786436
  160.4 66.3 %copy-start.8 = (bf16[128,64]{0,1:T(8,128)(2,1)S(1)}, bf16[128,64]{0,1:T(8,128)(2,1)}, u32[]{:S(2)}) copy-start(bf16[128,64]{0,1:T(8,128)(2,1)} %param.21) | copy-start | bytes 49156
  244.3 3.3 copy-start.6
  246.9 0.7 copy-start.2
  270.7 3.3 copy-start.6
  273.3 0.7 copy-start.2
  297.1 3.3 copy-start.6
  299.6 0.7 copy-start.2
  323.4 3.3 copy-start.6
  326.0 0.7 copy-start.2
  349.8 3.3 copy-start.6
  352.4 0.7 copy-start.2
  376.1 3.3 copy-start.6
  378.7 0.7 copy-start.2
  421.7 60.3 %copy-start.9 = (s32[48,192]{1,0:T(8,128)S(1)}, s32[48,192]{1,0:T(8,128)}, u32[]{:S(2)}) copy-start(s32[48,192]{1,0:T(8,128)} %param.15) | copy-start | bytes 110596
  421.7 60.4 %copy-start.4 = (bf16[6,8,12288]{2,1,0:T(8,128)(2,1)S(1)}, bf16[6,8,12288]{2,1,0:T(8,128)(2,1)}, u32[]{:S(2)}) copy-start(bf16[6,8,12288]{2,1,0:T(8,128)(2,1)} %get-tuple-element.106) | copy-start | bytes 3538948
  472.4 44.7 %all-to-all-start.2 = ((bf16[1,32,6,3072]{3,2,0,1:T(8,128)(2,1)}), bf16[1,32,6,3072]{3,2,0,1:T(8,128)(2,1)}, u32[]{:S(2)}, u32[]{:S(2)}) async-start(bf16[1,32,6,3072]{3,2,0,1:T(8,128)(2,1)} %bitcast.20), calls=%async_computation.2 | async-start | bytes 3145728 | tf_op jit(solution)/shard_map/all_to_all | solution.py:38
  522.4 3.6 slice-start
  522.4 3.7 slice-start.1
  547.9 8.4 %copy-start.7 = (bf16[128,512]{1,0:T(8,128)(2,1)S(1)}, bf16[128,512]{1,0:T(8,128)(2,1)}, u32[]{:S(2)}) copy-start(bf16[128,512]{1,0:T(8,128)(2,1)} %get-tuple-element.426) | copy-start | bytes 393220
  547.9 8.4 %copy-start.10 = (bf16[512,128]{1,0:T(8,128)(2,1)S(1)}, bf16[512,128]{1,0:T(8,128)(2,1)}, u32[]{:S(2)}) copy-start(bf16[512,128]{1,0:T(8,128)(2,1)} %get-tuple-element.433) | copy-start | bytes 393220
  610.7 0.8 copy-start.1
Sparse Core Ops, SparseCore 0:
  10.8 134.4 all-gather.1
  162.5 64.1 all-reduce.1
where the time goes:
time: 621 us; the launch traced here: 618 us
  waiting for transfers between devices  229 us (37%)
  local copies, waits for them, and re-layouts  148 us (24%)
  blocking collectives  85 us (14%)
  matrix products  78 us (13%)
  other arithmetic  55.8 us (9%)
  between operations  13.7 us (2%)
  starting transfers between devices  7.75 us (1%)
    all_gather x1, waiting for transfers between devices, per_device(): lax.all_gather(alignment, 'row', axis=0, tiled=True)  138 us
    convert_element_type x12, local copies, waits for them, and re-layouts, forward_block(): outer.reshape(block_rows * cols_dev, FACTOR_CHANNELS * FACTOR_CHANNELS)  64.8 us
    psum x1, waiting for transfers between devices, from_root(): return lax.psum(jnp.where(mine, shard, jnp.zeros_like(shard)), axis)  62.7 us
    all_to_all x1, blocking collectives, mirrored(): lax.all_to_all(regrouped, 'row', split_axis=0, concat_axis=1, tiled=True)  50.7 us
    all_to_all x1, blocking collectives, mirrored(): lax.all_to_all(sectioned, 'col', split_axis=0, concat_axis=0, tiled=True)  34.3 us
    convert_element_type x6, local copies, waits for them, and re-layouts, per_device(): scores = own.astype(jnp.float32) + across.astype(jnp.float32)  27.8 us
    all_to_all x1, waiting for transfers between devices, mirrored(): lax.all_to_all(lax.all_to_all(regrouped, 'row', split_axis=0, concat_axis...  27.8 us
    dot_general x6, matrix products, backward_block(): jnp.dot(dhidden, w_expand.T, preferred_element_type=jnp.float32)  17.7 us
  transfers between devices with their start and end apart: 3, of which 3 were waited for; matrix products, arithmetic and copies ran while one was open for 2% of the time, Pallas kernels for 0%

commit v1 on v0

--- a/solution.py
+++ b/solution.py
@@ -54,7 +54,12 @@
     ratio = n_row // n_col
     row_index = lax.axis_index("row")
     col_index = lax.axis_index("col")
-    factors = norm_project(lax.all_gather(alignment, "row", axis=0, tiled=True), projection_weight)
+    factors = norm_project(
+        jnp.concatenate(
+            lax.all_to_all(jnp.stack([alignment] * lax.axis_size("row")), "row", 0, 0), axis=0
+        ),
+        projection_weight,
+    )
     factors = factors.reshape(SEQUENCE_COUNT, cols_dev, 2 * FACTOR_CHANNELS)
     right_side = factors[:, :, FACTOR_CHANNELS:]
     own_left = lax.dynamic_slice_in_dim(

time: 621 us -> 669 us (1.077)
  waiting for transfers between devices: 229 us -> 252 us
  starting transfers between devices: 7.75 us -> 22.3 us
  other arithmetic: 55.8 us -> 64.5 us
    all_gather x1 -> x0, waiting for transfers between devices: 138 us -> none  [per_device(): lax.all_gather(alignment, 'row', axis=0, tiled=True)]
    all_to_all x0 -> x1, waiting for transfers between devices: none -> 137 us  [per_device(): lax.all_to_all(jnp.stack([alignment] * lax.axis_size('row')), 'row', 0, 0)]
    psum x1, waiting for transfers between devices: 62.7 us -> 87.1 us  [from_root(): return lax.psum(jnp.where(mine, shard, jnp.zeros_like(shard)), axis)]
    all_to_all x0 -> x1, starting transfers between devices: none -> 14.6 us  [per_device(): lax.all_to_all(jnp.stack([alignment] * lax.axis_size('row')), 'row', 0, 0)]
    convert_element_type x0 -> x1, other arithmetic: none -> 7.13 us  [norm_project(): layer_normalize(shard_rows.astype(jnp.float32))[0].astype(jnp.bfloat16)]
where the time goes in v1:
time: 669 us; the launch traced here: 666 us
  waiting for transfers between devices  252 us (38%)
  local copies, waits for them, and re-layouts  152 us (23%)
  blocking collectives  85 us (13%)
  matrix products  74.9 us (11%)
  other arithmetic  64.5 us (10%)
  starting transfers between devices  22.3 us (3%)
  between operations  13.7 us (2%)
    all_to_all x1, waiting for transfers between devices, per_device(): lax.all_to_all(jnp.stack([alignment] * lax.axis_size('row')), 'row', 0, 0)  137 us
    psum x1, waiting for transfers between devices, from_root(): return lax.psum(jnp.where(mine, shard, jnp.zeros_like(shard)), axis)  87.1 us
    convert_element_type x12, local copies, waits for them, and re-layouts, forward_block(): outer.reshape(block_rows * cols_dev, FACTOR_CHANNELS * FACTOR_CHANNELS)  64.8 us
    all_to_all x1, blocking collectives, mirrored(): lax.all_to_all(regrouped, 'row', split_axis=0, concat_axis=1, tiled=True)  50.7 us
    all_to_all x1, blocking collectives, mirrored(): lax.all_to_all(sectioned, 'col', split_axis=0, concat_axis=0, tiled=True)  34.3 us
    convert_element_type x6, local copies, waits for them, and re-layouts, per_device(): scores = own.astype(jnp.float32) + across.astype(jnp.float32)  27.8 us
    all_to_all x1, waiting for transfers between devices, mirrored(): lax.all_to_all(lax.all_to_all(regrouped, 'row', split_axis=0, concat_axis...  27.8 us
    dot_general x6, matrix products, backward_block(): jnp.dot(dhidden, w_expand.T, preferred_element_type=jnp.float32)  17.7 us
  transfers between devices with their start and end apart: 3, of which 3 were waited for; matrix products, arithmetic and copies ran while one was open for 2% of the time, Pallas kernels for 0%

profile of v1, /device:TPU:1, one launch (start us, length us, event | category | flops | bytes accessed | tf_op | source)
XLA Modules:
  0.0 665.9 jit_solution(2175141602042465207)
XLA Ops:
  6.5 4.3 stack.2
  10.9 14.6 %all-to-all-start = ((bf16[32,2,192,256]{3,2,1,0:T(8,128)(2,1)}), bf16[32,2,192,256]{3,2,1,0:T(8,128)(2,1)}, u32[]{:S(2)}, u32[]{:S(2)}) async-start(bf16[32,2,192,256]{3,2,1,0:T(8,128)(2,1)} %stack.2), calls=%async_computation | async-start | bytes 12582912 | tf_op jit(solution)/shard_map/all_to_all | solution.py:59
  25.6 137.2 %all-to-all-done = bf16[32,2,192,256]{3,2,1,0:T(8,128)(2,1)} async-done(((bf16[32,2,192,256]{3,2,1,0:T(8,128)(2,1)}), bf16[32,2,192,256]{3,2,1,0:T(8,128)(2,1)}, u32[]{:S(2)}, u32[]{:S(2)}) %all-to-all-start) | async-done | bytes 6291488 | tf_op jit(solution)/shard_map/all_to_all | solution.py:59
  162.8 5.1 convert_reduce_fusion.2
  168.0 6.1 multiply_reduce_fusion
  174.2 7.1 %fusion.53 = bf16[64,192,256]{2,1,0:T(8,128)(2,1)S(1)} fusion(bf16[32,2,192,256]{3,2,1,0:T(8,128)(2,1)} %all-to-all-done, f32[64,192]{1,0:T(8,128)S(1)} %rsqrt.28, f32[64,192]{1,0:T(8,128)S(1)} %div.59), kind=kLoop, calls=%fused_computation.74 | loop fusion | flops 12582912 | bytes 12681216 | tf_op jit(solution)/shard_map/convert_element_type | solution.py:25
  187.3 87.1 %all-reduce.2.cloned.1.call-done = bf16[6,64,8,32]{1,3,2,0:T(8,128)(2,1)} async-done(((bf16[6,64,8,32]{1,3,2,0:T(8,128)(2,1)}), bf16[6,64,8,32]{1,3,2,0:T(8,128)(2,1)}) %all-reduce.2.cloned.1.call-update) | async-done | bytes 196624 | tf_op jit(solution)/shard_map/psum | solution.py:14
  274.3 158.3 %while.24 = (s32[]{:T(128)}, bf16[6,1536,128]{1,2,0:T(8,128)(2,1)}, bf16[6,1536,512]{2,1,0:T(8,128)(2,1)}, bf16[6,8,12288]{2,1,0:T(8,128)(2,1)}, bf16[6,8,192,12...) while((s32[]{:T(128)}, bf16[6,1536,128]{1,2,0:T(8,128)(2,1)}, ...), condition=%wide.region_6.7_spmd, body=%wide.region_3.6_spmd.sunk | while | flops 1043695104 | bytes 37036208 | solution.py:104
  274.3 2.5 fusion.99
  276.8 4.5 copy.80
  281.3 6.3 convert_element_type.281
  289.6 2.3 copy.79
  291.9 2.6 bitcast_dynamic-update-slice_fusion.4
  295.9 2.3 convolution_convert_fusion.6
  300.7 2.5 fusion.99
  303.2 4.5 copy.80
  307.7 6.3 convert_element_type.281
  316.0 2.3 copy.79
  318.3 2.6 bitcast_dynamic-update-slice_fusion.4
  322.2 2.3 convolution_convert_fusion.6
  327.1 2.5 fusion.99
  329.6 4.5 copy.80
  334.1 6.3 convert_element_type.281
  342.4 2.3 copy.79
  344.7 2.6 bitcast_dynamic-update-slice_fusion.4
  348.6 2.3 convolution_convert_fusion.6
  353.5 2.5 fusion.99
  356.0 4.5 copy.80
  360.4 6.3 convert_element_type.281
  368.7 2.3 copy.79
  371.0 2.6 bitcast_dynamic-update-slice_fusion.4
  374.9 2.3 convolution_convert_fusion.6
  379.8 2.5 fusion.99
  382.3 4.5 copy.80
  386.8 6.3 convert_element_type.281
  395.1 2.3 copy.79
  397.4 2.5 bitcast_dynamic-update-slice_fusion.4
  401.3 2.3 convolution_convert_fusion.6
  406.2 2.5 fusion.99
  408.7 4.5 copy.80
  413.2 6.3 convert_element_type.281
  421.5 2.3 copy.79
  423.8 2.6 bitcast_dynamic-update-slice_fusion.4
  427.7 2.3 convolution_convert_fusion.6
  434.6 34.3 %all_to_all.31 = bf16[8,4,6,3072]{3,1,2,0:T(4,128)(2,1)S(1)} all-to-all(bf16[8,4,6,3072]{3,1,2,0:T(4,128)(2,1)S(1)} %bitcast.147), channel_id=1, replica_groups=mesh['row'=32,'col'=8] {'col'}, dimensions={0} | all-to-all | bytes 2359296 | tf_op jit(solution)/shard_map/all_to_all | solution.py:36
  469.3 50.7 %all_to_all.32 = bf16[32,1,6,3072]{3,2,1,0:T(8,128)(2,1)} all-to-all(bf16[32,1,6,3072]{3,2,1,0:T(8,128)(2,1)S(1)} %bitcast.146), channel_id=1, replica_groups=mesh['row'=32,'col'=8] {'row'}, dimensions={0} | all-to-all | bytes 2359296 | tf_op jit(solution)/shard_map/all_to_all | solution.py:39
  520.1 7.7 %all-to-all-start.3 = ((bf16[1,32,6,3072]{3,2,0,1:T(8,128)(2,1)}), bf16[1,32,6,3072]{3,2,0,1:T(8,128)(2,1)}, u32[]{:S(2)}, u32[]{:S(2)}) async-start(bf16[1,32,6,3072]{3,2,0,1:T(8,128)(2,1)} %bitcast.21), calls=%async_computation.3 | async-start | bytes 3145728 | tf_op jit(solution)/shard_map/all_to_all | solution.py:38
  529.8 3.6 reshape.162
  533.4 3.5 reshape.160
  536.9 27.8 %all-to-all-done.3 = bf16[1,32,6,3072]{3,2,0,1:T(8,128)(2,1)} async-done(((bf16[1,32,6,3072]{3,2,0,1:T(8,128)(2,1)}), bf16[1,32,6,3072]{3,2,0,1:T(8,128)(2,1)}, u32[]{:S(2)}, u32[]{:S(2)}) %all-to-all-start.3) | async-done | bytes 1179680 | tf_op jit(solution)/shard_map/all_to_all | solution.py:38
  566.8 3.2 reshape.164
  570.0 3.0 copy.60
  573.7 2.4 fusion.54
  576.2 4.7 exponential_reduce_fusion
  580.9 7.9 %copy.59 = f32[48,4,8,6,64]{4,3,2,1,0:T(8,128)} copy(f32[48,4,8,6,64]{4,0,1,2,3:T(8,128)} %bitcast.145) | data formatting | bytes 4718592 | tf_op jit(solution)/shard_map/convert_element_type | solution.py:109
  588.9 6.6 reshape.161
  595.5 8.4 %multiply_convert_fusion.1 = bf16[6,1536,64]{2,1,0:T(8,128)(2,1)} fusion(f32[6,1536,64]{2,1,0:T(8,128)} %reshape.160, f32[6,1536,64]{2,1,0:T(8,128)} %reshape.161, f32[6,1536]{1,0:T(8,128)S(1)} %multiply_multiply_fusion, s32[6,1536]{1,0:T(8,128)S(1)} %eq.22, f32[6,1536]{1,0:T(8,128)S(1)} %div.61, f32[6,1536]{1,0:T(8,128)S(1)} %sub.71), kind=kLoop, calls=%fused_computation.78 | loop fusion | flops 4718592 | bytes 6045696 | tf_op jit(solution)/shard_map/convert_element_type | solution.py:121
  603.9 54.4 %while.25 = (s32[]{:T(128)}, bf16[6,1536,128]{2,1,0:T(8,128)(2,1)}, bf16[6,1536,64]{2,1,0:T(8,128)(2,1)}, bf16[128,64]{0,1:T(8,128)(2,1)S(1)}, bf16[6,1536,128]{...) while((s32[]{:T(128)}, bf16[6,1536,128]{2,1,0:T(8,128)(2,1)}, ...), condition=%wide.region_14.15_spmd, body=%wide.region_9.14_spmd.sunk | while | flops 440010240 | bytes 12193377 | solution.py:148
  607.4 2.9 fusion.107
  616.4 3.0 fusion.107
  625.4 2.9 fusion.107
  634.4 3.0 fusion.107
  643.4 2.9 fusion.107
  652.5 3.0 fusion.107
  (206 shorter events, 85.3 us)
Async XLA Ops:
  6.5 174.8 %copy-start = (bf16[256,64]{0,1:T(8,128)(2,1)S(1)}, bf16[256,64]{0,1:T(8,128)(2,1)}, u32[]{:S(2)}) copy-start(bf16[256,64]{0,1:T(8,128)(2,1)} %param.17) | copy-start | bytes 98308
  10.9 151.9 %all-to-all-start = ((bf16[32,2,192,256]{3,2,1,0:T(8,128)(2,1)}), bf16[32,2,192,256]{3,2,1,0:T(8,128)(2,1)}, u32[]{:S(2)}, u32[]{:S(2)}) async-start(bf16[32,2,192,256]{3,2,1,0:T(8,128)(2,1)} %stack.2), calls=%async_computation | async-start | bytes 12582912 | tf_op jit(solution)/shard_map/all_to_all | solution.py:59
  25.5 248.8 %all-reduce.2.cloned.1.call-start = ((), (), s32[]{:S(2)}) async-start(), calls=%async_computation.4 | async-start | bytes 786432 | tf_op jit(solution)/shard_map/psum | solution.py:14
  183.7 90.6 %copy-start.4 = (bf16[1024,128]{1,0:T(8,128)(2,1)S(1)}, bf16[1024,128]{1,0:T(8,128)(2,1)}, u32[]{:S(2)}) copy-start(bf16[1024,128]{1,0:T(8,128)(2,1)} %param.18) | copy-start | bytes 786436
  183.7 90.6 %copy-start.7 = (bf16[128,64]{0,1:T(8,128)(2,1)S(1)}, bf16[128,64]{0,1:T(8,128)(2,1)}, u32[]{:S(2)}) copy-start(bf16[128,64]{0,1:T(8,128)(2,1)} %param.21) | copy-start | bytes 49156
  291.9 3.3 copy-start.5
  294.5 0.7 copy-start.2
  318.3 3.3 copy-start.5
  320.9 0.7 copy-start.2
  344.7 3.3 copy-start.5
  347.3 0.7 copy-start.2
  371.0 3.3 copy-start.5
  373.6 0.7 copy-start.2
  397.4 3.3 copy-start.5
  400.0 0.7 copy-start.2
  423.8 3.3 copy-start.5
  426.3 0.7 copy-start.2
  469.3 60.3 %copy-start.8 = (s32[48,192]{1,0:T(8,128)S(1)}, s32[48,192]{1,0:T(8,128)}, u32[]{:S(2)}) copy-start(s32[48,192]{1,0:T(8,128)} %param.15) | copy-start | bytes 110596
  469.3 60.4 %copy-start.3 = (bf16[6,8,12288]{2,1,0:T(8,128)(2,1)S(1)}, bf16[6,8,12288]{2,1,0:T(8,128)(2,1)}, u32[]{:S(2)}) copy-start(bf16[6,8,12288]{2,1,0:T(8,128)(2,1)} %get-tuple-element.106) | copy-start | bytes 3538948
  520.1 44.7 %all-to-all-start.3 = ((bf16[1,32,6,3072]{3,2,0,1:T(8,128)(2,1)}), bf16[1,32,6,3072]{3,2,0,1:T(8,128)(2,1)}, u32[]{:S(2)}, u32[]{:S(2)}) async-start(bf16[1,32,6,3072]{3,2,0,1:T(8,128)(2,1)} %bitcast.21), calls=%async_computation.3 | async-start | bytes 3145728 | tf_op jit(solution)/shard_map/all_to_all | solution.py:38
  570.0 3.6 slice-start
  570.0 3.7 slice-start.1
  595.5 8.4 %copy-start.6 = (bf16[128,512]{1,0:T(8,128)(2,1)S(1)}, bf16[128,512]{1,0:T(8,128)(2,1)}, u32[]{:S(2)}) copy-start(bf16[128,512]{1,0:T(8,128)(2,1)} %get-tuple-element.426) | copy-start | bytes 393220
  595.5 8.4 %copy-start.9 = (bf16[512,128]{1,0:T(8,128)(2,1)S(1)}, bf16[512,128]{1,0:T(8,128)(2,1)}, u32[]{:S(2)}) copy-start(bf16[512,128]{1,0:T(8,128)(2,1)} %get-tuple-element.431) | copy-start | bytes 393220
  658.3 0.8 copy-start.1
Sparse Core Ops, SparseCore 0:
  185.8 88.4 all-reduce.1
